TPU v7x, 32 devices: a whole 2x2x4 slice. The times are simulated.
32 devices in a mesh: dp: 8 (over z, core), expert: 4 (over y, x).
Axes of the slice: x: 2, y: 2, z: 4, core: 2. Of those that a mesh axis runs over, the one named last changes fastest.
Arguments:
- embedded: bfloat16 [64, 197, 512], P(('dp', 'expert')), may hold values from -6 to 6
- cotangent: bfloat16 [64, 197, 512], P(('dp', 'expert')), may hold values from -6 to 6
- w_qkv: bfloat16 [2, 512, 1536], P(None, 'dp'), may hold values from -0.25 to 0.25
- w_proj: bfloat16 [2, 512, 512], P(None, 'dp'), may hold values from -2.5 to 2.5
- w_router: bfloat16 [2, 512, 8], P(None, 'dp'), may hold values from -0.1875 to 0.1875
- norm_gains: bfloat16 [2, 2, 512], P(None, None, 'dp'), may hold values from 0.25 to 1.75
- norm_shifts: bfloat16 [2, 2, 512], P(None, None, 'dp'), may hold values from -1 to 1
- w_first: bfloat16 [2, 8, 512, 2048], P(None, 'expert', None, 'dp'), may hold values from -0.25 to 0.25
- w_second: bfloat16 [2, 8, 2048, 512], P(None, 'expert', 'dp'), may hold values from -1 to 1
- routes: int32 [2, 64, 197, 2], P(None, ('dp', 'expert')), may hold values from 0 to 7, all different within a row; in each aligned block of 394 rows (0 to 393, 394 to 787, ..., all dimensions but the last counted through in order) at most 147 rows name the same one
Outputs:
- out_images: bfloat16 [64, 197, 512], P(('dp', 'expert'))
- grad_images: float32 [64, 197, 512], P(('dp', 'expert'))
- grad_qkv: float32 [2, 512, 1536], P(None, 'dp')
- grad_proj: float32 [2, 512, 512], P(None, 'dp')
- grad_router: float32 [2, 512, 8], P(None, 'dp')
- grad_gains: float32 [2, 2, 512], P(None, None, 'dp')
- grad_shifts: float32 [2, 2, 512], P(None, None, 'dp')
- grad_first: float32 [2, 8, 512, 2048], P(None, 'expert', None, 'dp')
- grad_second: float32 [2, 8, 2048, 512], P(None, 'expert', 'dp')
Inputs may be any that keep to these rules, and one draw needn't show every extreme that they name: `routes`: the two experts of a token differ. Among the 394 tokens of one device in one block, no expert is named by more than 147 tokens, a bound that some block reaches.
All inputs are finite; a program needn't handle non-finite values.
Results may differ from a plain program's by a relative error of at most 0.019.
Values may be sent and summed in bfloat16 or wider, within the bound.
No kernel may reach another device: no remote copies, remote signals or barrier semaphores. Data moves between devices by JAX's collectives and lax.ppermute only.
A program may use at most 192 MiB of HBM per device.

v0:
```python
import jax
import jax.numpy as jnp
from jax import lax
from jax.sharding import PartitionSpec as P

HEADS = 8
HEAD_DIM = 64
SEQ = 197
LAYERS = 2
EPSILON = 1e-06
ROOT_HALF = 0.7071067811865476
INV_ROOT_TAU = 0.3989422804014327


def layer_norm(values, scale_in, shift_in):
    center = values - jnp.mean(values, axis=-1, keepdims=True)
    variance = jnp.mean(center * center, axis=-1, keepdims=True)
    inverse = lax.rsqrt(variance + EPSILON)
    normed = center * inverse
    return (normed * scale_in + shift_in, normed, inverse)


def norm_back(grad_out, normed, inverse, scale_in):
    grad_normed = grad_out * scale_in
    first_mean = jnp.mean(grad_normed, axis=-1, keepdims=True)
    second_mean = jnp.mean(grad_normed * normed, axis=-1, keepdims=True)
    grad_in = inverse * (grad_normed - first_mean - normed * second_mean)
    return (grad_in, jnp.sum(grad_out * normed, axis=0), jnp.sum(grad_out, axis=0))


def softmax_rows(scores):
    highest = jnp.max(scores, axis=-1, keepdims=True)
    powers = jnp.exp(scores - highest)
    row_total = jnp.sum(powers, axis=-1, keepdims=True)
    return (powers / row_total, highest + jnp.log(row_total))


def gelu_value(preact):
    return 0.5 * preact * (1.0 + lax.erf(preact * ROOT_HALF))


def gelu_slope(preact):
    return (
        0.5 * (1.0 + lax.erf(preact * ROOT_HALF))
        + preact * jnp.exp(-0.5 * preact * preact) * INV_ROOT_TAU
    )


def layer_forward(
    resid, which, w_qkv, w_proj, w_router, norm_gains, norm_shifts, w_first, w_second, routes
):
    qkv_full, proj_full, router_full, gains_full, shifts_full = (
        lax.all_gather(w_qkv[which], "dp", axis=0, tiled=True),
        lax.all_gather(w_proj[which], "dp", axis=0, tiled=True),
        lax.all_gather(w_router[which], "dp", axis=0, tiled=True),
        lax.all_gather(norm_gains[which], "dp", axis=1, tiled=True),
        lax.all_gather(norm_shifts[which], "dp", axis=1, tiled=True),
    )
    first_full, second_full = (
        lax.all_gather(w_first[which], "dp", axis=2, tiled=True),
        lax.all_gather(w_second[which], "dp", axis=1, tiled=True),
    )
    tok_count, width = resid.shape
    images = tok_count // SEQ
    gains_wide = gains_full.astype(jnp.float32)
    shifts_wide = shifts_full.astype(jnp.float32)
    attn_norm, unit_a, inv_a = layer_norm(resid, gains_wide[0], shifts_wide[0])
    attn_in = attn_norm.astype(jnp.bfloat16)
    packed = jnp.dot(attn_in, qkv_full, preferred_element_type=jnp.float32)
    head_shape = (images, SEQ, HEADS, HEAD_DIM)
    query = (packed[:, :width] * HEAD_DIM ** (-0.5)).astype(jnp.bfloat16).reshape(head_shape)
    keyed = packed[:, width : 2 * width].astype(jnp.bfloat16).reshape(head_shape)
    valued = packed[:, 2 * width :].astype(jnp.bfloat16).reshape(head_shape)
    scores = jnp.einsum("iqhd,ikhd->ihqk", query, keyed, preferred_element_type=jnp.float32)
    probs, log_total = softmax_rows(scores)
    mixed = jnp.einsum(
        "ihqk,ikhd->iqhd", probs.astype(jnp.bfloat16), valued, preferred_element_type=jnp.float32
    )
    mixed = mixed.reshape(tok_count, width).astype(jnp.bfloat16)
    resid_mid = resid + jnp.dot(mixed, proj_full, preferred_element_type=jnp.float32)
    moe_norm, unit_b, inv_b = layer_norm(resid_mid, gains_wide[1], shifts_wide[1])
    moe_in = moe_norm.astype(jnp.bfloat16)
    logits = jnp.dot(moe_in, router_full, preferred_element_type=jnp.float32)
    router_probs, ignored_total = softmax_rows(logits)
    experts_total = router_full.shape[1]
    local_count = first_full.shape[0]
    peers = lax.axis_size("expert")
    capacity = max(2, 3 * tok_count // experts_total)
    route = routes[which].reshape(tok_count, 2)
    labels = jnp.arange(experts_total, dtype=jnp.int32)
    pick_first = (route[:, 0:1] == labels[None, :]).astype(jnp.int32)
    pick_second = (route[:, 1:2] == labels[None, :]).astype(jnp.int32)
    both_picks = pick_first + pick_second
    before = jnp.cumsum(both_picks, axis=0) - both_picks
    slot_first = route[:, 0] * capacity + jnp.sum(before * pick_first, axis=1)
    slot_second = route[:, 1] * capacity + jnp.sum(before * pick_second, axis=1)
    slot_ids = jnp.arange(experts_total * capacity, dtype=jnp.int32)
    place_first = (slot_ids[:, None] == slot_first[None, :]).astype(jnp.bfloat16)
    place_second = (slot_ids[:, None] == slot_second[None, :]).astype(jnp.bfloat16)
    outgoing = jnp.dot(place_first + place_second, moe_in, preferred_element_type=jnp.float32)
    outgoing = outgoing.astype(jnp.bfloat16).reshape(peers, local_count, capacity, width)
    incoming = lax.all_to_all(outgoing, "expert", split_axis=0, concat_axis=0, tiled=True)
    hidden_pre = jnp.einsum(
        "sjcd,jdf->sjcf", incoming, first_full, preferred_element_type=jnp.float32
    )
    hidden_act = gelu_value(hidden_pre).astype(jnp.bfloat16)
    result = jnp.einsum(
        "sjcf,jfd->sjcd", hidden_act, second_full, preferred_element_type=jnp.float32
    ).astype(jnp.bfloat16)
    returned = lax.all_to_all(result, "expert", split_axis=0, concat_axis=0, tiled=True).reshape(
        experts_total * capacity, width
    )
    pick_first_f = pick_first.astype(jnp.float32)
    pick_second_f = pick_second.astype(jnp.float32)
    gate_first = jnp.sum(router_probs * pick_first_f, axis=1)
    gate_second = jnp.sum(router_probs * pick_second_f, axis=1)
    back_first = jnp.take(returned, slot_first, axis=0).astype(jnp.float32)
    back_second = jnp.take(returned, slot_second, axis=0).astype(jnp.float32)
    resid_out = resid_mid + (gate_first[:, None] * back_first + gate_second[:, None] * back_second)
    saved = (
        qkv_full,
        proj_full,
        router_full,
        gains_wide,
        first_full,
        second_full,
        unit_a,
        inv_a,
        attn_in,
        query,
        keyed,
        valued,
        log_total,
        mixed,
        unit_b,
        inv_b,
        moe_in,
        router_probs,
        pick_first_f,
        pick_second_f,
        slot_first,
        slot_second,
        place_first,
        place_second,
        incoming,
        hidden_pre,
        hidden_act,
        returned,
        gate_first,
        gate_second,
    )
    return (resid_out, saved)


def layer_backward(grad_out, saved):
    (
        qkv_full,
        proj_full,
        router_full,
        gains_wide,
        first_full,
        second_full,
        unit_a,
        inv_a,
        attn_in,
        query,
        keyed,
        valued,
        log_total,
        mixed,
        unit_b,
        inv_b,
        moe_in,
        router_probs,
        pick_first_f,
        pick_second_f,
        slot_first,
        slot_second,
        place_first,
        place_second,
        incoming,
        hidden_pre,
        hidden_act,
        returned,
        gate_first,
        gate_second,
    ) = saved
    tok_count, width = grad_out.shape
    images = tok_count // SEQ
    back_first = jnp.take(returned, slot_first, axis=0).astype(jnp.float32)
    back_second = jnp.take(returned, slot_second, axis=0).astype(jnp.float32)
    grad_gate_first = jnp.sum(grad_out * back_first, axis=1)
    grad_gate_second = jnp.sum(grad_out * back_second, axis=1)
    send_first = (gate_first[:, None] * grad_out).astype(jnp.bfloat16)
    send_second = (gate_second[:, None] * grad_out).astype(jnp.bfloat16)
    slot_grads = jnp.dot(place_first, send_first, preferred_element_type=jnp.float32) + jnp.dot(
        place_second, send_second, preferred_element_type=jnp.float32
    )
    slot_grads = slot_grads.astype(jnp.bfloat16).reshape(incoming.shape)
    grad_result = lax.all_to_all(slot_grads, "expert", split_axis=0, concat_axis=0, tiled=True)
    grad_act = jnp.einsum(
        "sjcd,jfd->sjcf", grad_result, second_full, preferred_element_type=jnp.float32
    )
    grad_second = jnp.einsum(
        "sjcf,sjcd->jfd", hidden_act, grad_result, preferred_element_type=jnp.float32
    )
    grad_pre = (grad_act * gelu_slope(hidden_pre)).astype(jnp.bfloat16)
    grad_first = jnp.einsum(
        "sjcd,sjcf->jdf", incoming, grad_pre, preferred_element_type=jnp.float32
    )
    grad_rows = jnp.einsum(
        "sjcf,jdf->sjcd", grad_pre, first_full, preferred_element_type=jnp.float32
    ).astype(jnp.bfloat16)
    grad_back = lax.all_to_all(
        grad_rows, "expert", split_axis=0, concat_axis=0, tiled=True
    ).reshape(-1, width)
    grad_moe = jnp.einsum(
        "st,sd->td", place_first + place_second, grad_back, preferred_element_type=jnp.float32
    )
    grad_probs = pick_first_f * grad_gate_first[:, None] + pick_second_f * grad_gate_second[:, None]
    weighted = jnp.sum(router_probs * grad_probs, axis=1, keepdims=True)
    grad_logits = (router_probs * (grad_probs - weighted)).astype(jnp.bfloat16)
    grad_router = jnp.einsum("td,te->de", moe_in, grad_logits, preferred_element_type=jnp.float32)
    grad_moe = grad_moe + jnp.einsum(
        "te,de->td", grad_logits, router_full, preferred_element_type=jnp.float32
    )
    grad_norm_b, gain_b_grad, shift_b_grad = norm_back(grad_moe, unit_b, inv_b, gains_wide[1])
    grad_mid = grad_out + grad_norm_b
    grad_branch = grad_mid.astype(jnp.bfloat16)
    grad_proj = jnp.einsum("td,te->de", mixed, grad_branch, preferred_element_type=jnp.float32)
    grad_mixed = jnp.einsum("te,de->td", grad_branch, proj_full, preferred_element_type=jnp.float32)
    grad_mixed = grad_mixed.astype(jnp.bfloat16).reshape(images, SEQ, HEADS, HEAD_DIM)
    scores = jnp.einsum("iqhd,ikhd->ihqk", query, keyed, preferred_element_type=jnp.float32)
    probs = jnp.exp(scores - log_total)
    grad_weights = jnp.einsum(
        "iqhd,ikhd->ihqk", grad_mixed, valued, preferred_element_type=jnp.float32
    )
    grad_valued = jnp.einsum(
        "ihqk,iqhd->ikhd",
        probs.astype(jnp.bfloat16),
        grad_mixed,
        preferred_element_type=jnp.float32,
    ).astype(jnp.bfloat16)
    row_inner = jnp.sum(probs * grad_weights, axis=-1, keepdims=True)
    grad_scores = (probs * (grad_weights - row_inner)).astype(jnp.bfloat16)
    grad_query = jnp.einsum(
        "ihqk,ikhd->iqhd", grad_scores, keyed, preferred_element_type=jnp.float32
    ).astype(jnp.bfloat16)
    grad_query = grad_query * jnp.asarray(HEAD_DIM ** (-0.5), jnp.bfloat16)
    grad_keyed = jnp.einsum(
        "ihqk,iqhd->ikhd", grad_scores, query, preferred_element_type=jnp.float32
    ).astype(jnp.bfloat16)
    grad_packed = jnp.concatenate(
        [
            grad_query.reshape(tok_count, width),
            grad_keyed.reshape(tok_count, width),
            grad_valued.reshape(tok_count, width),
        ],
        axis=1,
    )
    grad_qkv = jnp.einsum("td,te->de", attn_in, grad_packed, preferred_element_type=jnp.float32)
    grad_attn = jnp.einsum("te,de->td", grad_packed, qkv_full, preferred_element_type=jnp.float32)
    grad_norm_a, gain_a_grad, shift_a_grad = norm_back(grad_attn, unit_a, inv_a, gains_wide[0])
    grad_in = grad_mid + grad_norm_a
    dense = (
        grad_qkv,
        grad_proj,
        grad_router,
        jnp.stack([gain_a_grad, gain_b_grad]),
        jnp.stack([shift_a_grad, shift_b_grad]),
    )
    return (grad_in, dense, (grad_first, grad_second))


def body(
    embedded, cotangent, w_qkv, w_proj, w_router, norm_gains, norm_shifts, w_first, w_second, routes
):
    images, length, width = embedded.shape
    tok_count = images * length
    resid = embedded.reshape(tok_count, width).astype(jnp.float32)
    layer_inputs = []
    for which in range(LAYERS):
        layer_inputs.append(resid)
        resid, saved = layer_forward(
            resid,
            which,
            w_qkv,
            w_proj,
            w_router,
            norm_gains,
            norm_shifts,
            w_first,
            w_second,
            routes,
        )
    out_images = resid.reshape(images, length, width).astype(jnp.bfloat16)
    grad = cotangent.reshape(tok_count, width).astype(jnp.float32)
    dense_layers = []
    expert_layers = []
    for which in reversed(range(LAYERS)):
        ignored, saved = layer_forward(
            layer_inputs[which],
            which,
            w_qkv,
            w_proj,
            w_router,
            norm_gains,
            norm_shifts,
            w_first,
            w_second,
            routes,
        )
        grad, dense, expert_part = layer_backward(grad, saved)
        totals = (
            lax.psum(dense[0].astype(jnp.bfloat16), "expert").astype(jnp.float32),
            lax.psum(dense[1].astype(jnp.bfloat16), "expert").astype(jnp.float32),
            lax.psum(dense[2].astype(jnp.bfloat16), "expert").astype(jnp.float32),
            lax.psum(dense[3].astype(jnp.bfloat16), "expert").astype(jnp.float32),
            lax.psum(dense[4].astype(jnp.bfloat16), "expert").astype(jnp.float32),
        )
        shares = (
            lax.psum_scatter(
                totals[0].astype(jnp.bfloat16), "dp", scatter_dimension=0, tiled=True
            ).astype(jnp.float32),
            lax.psum_scatter(
                totals[1].astype(jnp.bfloat16), "dp", scatter_dimension=0, tiled=True
            ).astype(jnp.float32),
            lax.psum_scatter(
                totals[2].astype(jnp.bfloat16), "dp", scatter_dimension=0, tiled=True
            ).astype(jnp.float32),
            lax.psum_scatter(
                totals[3].astype(jnp.bfloat16), "dp", scatter_dimension=1, tiled=True
            ).astype(jnp.float32),
            lax.psum_scatter(
                totals[4].astype(jnp.bfloat16), "dp", scatter_dimension=1, tiled=True
            ).astype(jnp.float32),
        )
        expert_shares = (
            lax.psum_scatter(
                expert_part[0].astype(jnp.bfloat16), "dp", scatter_dimension=2, tiled=True
            ).astype(jnp.float32),
            lax.psum_scatter(
                expert_part[1].astype(jnp.bfloat16), "dp", scatter_dimension=1, tiled=True
            ).astype(jnp.float32),
        )
        dense_layers.insert(0, shares)
        expert_layers.insert(0, expert_shares)
    grad_images = grad.reshape(images, length, width)
    grad_qkv = jnp.stack([entry[0] for entry in dense_layers])
    grad_proj = jnp.stack([entry[1] for entry in dense_layers])
    grad_router = jnp.stack([entry[2] for entry in dense_layers])
    grad_gains = jnp.stack([entry[3] for entry in dense_layers])
    grad_shifts = jnp.stack([entry[4] for entry in dense_layers])
    grad_first = jnp.stack([entry[0] for entry in expert_layers])
    grad_second = jnp.stack([entry[1] for entry in expert_layers])
    return (
        out_images,
        grad_images,
        grad_qkv,
        grad_proj,
        grad_router,
        grad_gains,
        grad_shifts,
        grad_first,
        grad_second,
    )


def solution(mesh):
    return jax.shard_map(
        body,
        mesh=mesh,
        in_specs=(
            P(("dp", "expert"), None, None),
            P(("dp", "expert"), None, None),
            P(None, "dp", None),
            P(None, "dp", None),
            P(None, "dp", None),
            P(None, None, "dp"),
            P(None, None, "dp"),
            P(None, "expert", None, "dp"),
            P(None, "expert", "dp", None),
            P(None, ("dp", "expert"), None, None),
        ),
        out_specs=(
            P(("dp", "expert"), None, None),
            P(("dp", "expert"), None, None),
            P(None, "dp", None),
            P(None, "dp", None),
            P(None, "dp", None),
            P(None, None, "dp"),
            P(None, None, "dp"),
            P(None, "expert", None, "dp"),
            P(None, "expert", "dp", None),
        ),
        check_vma=False,
    )
```

profile of v0, /device:TPU:0, one launch (start us, length us, event | category | flops | bytes accessed | tf_op | source)
XLA Modules:
  0.0 1092.9 jit_solution(856967177096205174)
XLA Ops:
  16.5 17.0 %all-gather = bf16[1,2,512]{1,0,2:T(2,128)(2,1)S(1)} all-gather(bf16[1,2,64]{1,0,2:T(2,128)(2,1)S(1)} %copy.377), channel_id=2, replica_groups=mesh['dp'=8,'expert'=4] {'dp'}, dimensions={2}, use_global_device_ids=true | all-gather | bytes 2304 | tf_op jit(solution)/shard_map/all_gather | solution.py:56
  37.7 14.6 %all-gather.1 = bf16[1,2,512]{1,0,2:T(2,128)(2,1)S(1)} all-gather(bf16[1,2,64]{1,0,2:T(2,128)(2,1)S(1)} %copy.378), channel_id=3, replica_groups=mesh['dp'=8,'expert'=4] {'dp'}, dimensions={2}, use_global_device_ids=true | all-gather | bytes 2304 | tf_op jit(solution)/shard_map/all_gather | solution.py:57
  55.9 25.2 %all-gather.3 = bf16[1,512,512]{2,1,0:T(8,128)(2,1)} all-gather(bf16[1,64,512]{2,1,0:T(8,128)(2,1)S(1)} %get-tuple-element.126), channel_id=5, replica_groups=mesh['dp'=8,'expert'=4] {'dp'}, dimensions={1}, use_global_device_ids=true | all-gather | bytes 589824 | tf_op jit(solution)/shard_map/all_gather | solution.py:54
  118.6 4.3 all-to-all-start
  122.9 15.7 %all-gather.4 = bf16[1,512,8]{2,0,1:T(2,128)(2,1)S(1)} all-gather(bf16[1,64,8]{2,0,1:T(2,128)(2,1)} %copy.379), channel_id=6, replica_groups=mesh['dp'=8,'expert'=4] {'dp'}, dimensions={1}, use_global_device_ids=true | all-gather | bytes 9216 | tf_op jit(solution)/shard_map/all_gather | solution.py:55
  140.0 14.2 %all-gather.7 = bf16[1,2,512]{1,0,2:T(2,128)(2,1)S(1)} all-gather(bf16[1,2,64]{1,0,2:T(2,128)(2,1)S(1)} %copy.380), channel_id=9, replica_groups=mesh['dp'=8,'expert'=4] {'dp'}, dimensions={2}, use_global_device_ids=true | all-gather | bytes 2304 | tf_op jit(solution)/shard_map/all_gather | solution.py:56
  155.8 15.6 %all-gather.8 = bf16[1,2,512]{1,0,2:T(2,128)(2,1)S(1)} all-gather(bf16[1,2,64]{1,0,2:T(2,128)(2,1)} %copy.381), channel_id=10, replica_groups=mesh['dp'=8,'expert'=4] {'dp'}, dimensions={2}, use_global_device_ids=true | all-gather | bytes 2304 | tf_op jit(solution)/shard_map/all_gather | solution.py:57
  183.4 9.1 fusion.17
  192.5 6.6 fusion.77
  201.4 4.3 all-to-all-start.1
  206.3 17.5 %all-gather.10 = bf16[1,512,512]{2,1,0:T(8,128)(2,1)} all-gather(bf16[1,64,512]{2,1,0:T(8,128)(2,1)S(1)} %copy-done.50), channel_id=12, replica_groups=mesh['dp'=8,'expert'=4] {'dp'}, dimensions={1}, use_global_device_ids=true | all-gather | bytes 589824 | tf_op jit(solution)/shard_map/all_gather | solution.py:54
  230.6 4.3 gather_fusion
  234.9 4.1 gather_fusion.1
  242.0 4.1 fusion.213
  282.2 4.3 all-to-all-start.2
  287.3 14.8 %all-gather.11 = bf16[1,512,8]{2,0,1:T(2,128)(2,1)S(1)} all-gather(bf16[1,64,8]{2,0,1:T(2,128)(2,1)} %copy.382), channel_id=13, replica_groups=mesh['dp'=8,'expert'=4] {'dp'}, dimensions={1}, use_global_device_ids=true | all-gather | bytes 9216 | tf_op jit(solution)/shard_map/all_gather | solution.py:55
  306.9 9.1 fusion.13
  316.0 6.4 fusion.83
  324.8 4.3 all-to-all-start.3
  330.4 15.1 %all-to-all-done.3 = bf16[4,2,147,512]{3,1,2,0:T(2,128)(2,1)} async-done(((bf16[4,2,147,512]{3,1,2,0:T(2,128)(2,1)}), bf16[4,2,147,512]{3,1,2,0:T(2,128)(2,1)}, u32[]{:S(2)}, u32[]{:S(2)}) %all-to-all-start.3) | async-done | bytes 1204256 | tf_op jit(solution)/shard_map/all_to_all | solution.py:110
  354.7 4.0 gather_fusion.2
  369.8 18.9 %all_to_all.44 = bf16[4,2,147,512]{3,1,2,0:T(2,128)(2,1)S(1)} all-to-all(bf16[4,2,147,512]{3,1,2,0:T(2,128)(2,1)S(1)} %copy.295), channel_id=1, replica_groups=mesh['dp'=8,'expert'=4] {'expert'}, dimensions={0} | all-to-all | bytes 2408448 | tf_op jit(solution)/shard_map/all_to_all | solution.py:200
  388.7 8.1 fusion.5
  401.8 4.3 all-to-all-start.5
  406.2 14.4 %all-to-all-done.5 = bf16[4,2,147,512]{3,1,2,0:T(2,128)(2,1)} async-done(((bf16[4,2,147,512]{3,1,2,0:T(2,128)(2,1)}), bf16[4,2,147,512]{3,1,2,0:T(2,128)(2,1)}, u32[]{:S(2)}, u32[]{:S(2)}) %all-to-all-start.5) | async-done | bytes 1204256 | tf_op jit(solution)/shard_map/all_to_all | solution.py:214
  471.1 18.4 %all_to_all.45 = bf16[4,2,147,512]{3,1,2,0:T(2,128)(2,1)S(1)} all-to-all(bf16[4,2,147,512]{3,1,2,0:T(2,128)(2,1)S(1)} %copy.311), channel_id=1, replica_groups=mesh['dp'=8,'expert'=4] {'expert'}, dimensions={0} | all-to-all | bytes 2408448 | tf_op jit(solution)/shard_map/all_to_all | solution.py:200
  489.5 8.1 fusion.11
  502.6 4.4 all-to-all-start.7
  509.8 11.1 %all-to-all-done.7 = bf16[4,2,147,512]{3,1,2,0:T(2,128)(2,1)} async-done(((bf16[4,2,147,512]{3,1,2,0:T(2,128)(2,1)}), bf16[4,2,147,512]{3,1,2,0:T(2,128)(2,1)}, u32[]{:S(2)}, u32[]{:S(2)}) %all-to-all-start.7) | async-done | bytes 1204256 | tf_op jit(solution)/shard_map/all_to_all | solution.py:214
  532.0 4.1 convolution_convert_fusion
  569.2 5.1 reduce-scatter.39.cloned.1.call-done
  574.3 35.1 %reduce-scatter.37.cloned.1.call-done = bf16[64,1536]{1,0:T(8,128)(2,1)} async-done(((bf16[512,1536]{1,0:T(8,128)(2,1)}), bf16[64,1536]{1,0:T(8,128)(2,1)}) %reduce-scatter.37.cloned.1.call-update) | async-done | bytes 196624 | tf_op jit(solution)/shard_map/reduce_scatter | solution.py:322
  609.4 34.7 %reduce-scatter.35.cloned.1.call-done = bf16[64,1536]{1,0:T(8,128)(2,1)} async-done(((bf16[512,1536]{1,0:T(8,128)(2,1)}), bf16[64,1536]{1,0:T(8,128)(2,1)}) %reduce-scatter.35.cloned.1.call-update) | async-done | bytes 196624 | tf_op jit(solution)/shard_map/reduce_scatter | solution.py:322
  644.4 8.4 bitcast_convert_fusion
  654.0 8.5 bitcast_convert_fusion.1
  662.6 8.4 bitcast_convert_fusion.2
  671.3 8.3 bitcast_convert_fusion.3
  681.8 25.0 %reduce-scatter.53.cloned.1.call-done = bf16[64,2]{1,0:T(8,128)(2,1)} async-done(((bf16[512,2]{1,0:T(8,128)(2,1)}), bf16[64,2]{1,0:T(8,128)(2,1)}) %reduce-scatter.53.cloned.1.call-update) | async-done | bytes 272
  707.6 30.8 %reduce-scatter.49.cloned.1.call-done = bf16[64,2]{1,0:T(8,128)(2,1)} async-done(((bf16[512,2]{1,0:T(8,128)(2,1)}), bf16[64,2]{1,0:T(8,128)(2,1)}) %reduce-scatter.49.cloned.1.call-update) | async-done | bytes 272
  739.2 30.7 %reduce-scatter.43.cloned.1.call-done = bf16[64,8]{1,0:T(8,128)(2,1)} async-done(((bf16[512,8]{1,0:T(8,128)(2,1)}), bf16[64,8]{1,0:T(8,128)(2,1)}) %reduce-scatter.43.cloned.1.call-update) | async-done | bytes 1040
  772.6 28.1 %reduce-scatter.51.cloned.1.call-done = bf16[64,2]{1,0:T(8,128)(2,1)} async-done(((bf16[512,2]{1,0:T(8,128)(2,1)}), bf16[64,2]{1,0:T(8,128)(2,1)}) %reduce-scatter.51.cloned.1.call-update) | async-done | bytes 272
  801.5 30.6 %reduce-scatter.47.cloned.1.call-done = bf16[64,2]{1,0:T(8,128)(2,1)} async-done(((bf16[512,2]{1,0:T(8,128)(2,1)}), bf16[64,2]{1,0:T(8,128)(2,1)}) %reduce-scatter.47.cloned.1.call-update) | async-done | bytes 272
  832.9 10.1 all-reduce.2
  844.7 34.3 %all-reduce.6.cloned.1.call-done = (bf16[64,1536]{1,0:T(8,128)(2,1)}, bf16[64,1536]{1,0:T(8,128)(2,1)}, bf16[64,512]{1,0:T(8,128)(2,1)}, bf16[64,512]{1,0:T(8,128)(2,1)}) async-done(((bf16[64,1536]{1,0:T(8,128)(2,1)}, bf16[64,1536]{1,0:T(8,128)(2,1)}, bf16[64,512]{1,0:T(8,128)(2,1)}, bf16[64,512]{1,0:T(8,128)(2,1)}), (bf16[64,1536]{1,0:T(8,128)(2,1)}, bf16[64,1536]{1,0:T(8,128)(2,1)}, ...) | async-done | bytes 524304 | tf_op jit(solution)/shard_map/psum | solution.py:315
  882.6 48.5 %reduce-scatter.33.cloned.1.call-done = bf16[2,256,512]{2,1,0:T(8,128)(2,1)} async-done(((bf16[2,2048,512]{2,1,0:T(8,128)(2,1)}), bf16[2,256,512]{2,1,0:T(8,128)(2,1)}) %reduce-scatter.33.cloned.1.call-update) | async-done | bytes 524304 | tf_op jit(solution)/shard_map/reduce_scatter | solution.py:342
  931.1 50.7 %reduce-scatter.31.cloned.1.call-done = bf16[2,256,512]{2,1,0:T(8,128)(2,1)} async-done(((bf16[2,2048,512]{2,1,0:T(8,128)(2,1)}), bf16[2,256,512]{2,1,0:T(8,128)(2,1)}) %reduce-scatter.31.cloned.1.call-update) | async-done | bytes 524304 | tf_op jit(solution)/shard_map/reduce_scatter | solution.py:342
  984.5 47.9 %reduce-scatter.29.cloned.1.call-done = bf16[2,512,256]{2,1,0:T(8,128)(2,1)} async-done(((bf16[2,512,2048]{2,1,0:T(8,128)(2,1)}), bf16[2,512,256]{2,1,0:T(8,128)(2,1)}) %reduce-scatter.29.cloned.1.call-update) | async-done | bytes 524304 | tf_op jit(solution)/shard_map/reduce_scatter | solution.py:339
  1032.4 50.7 %reduce-scatter.27.cloned.1.call-done = bf16[2,512,256]{2,1,0:T(8,128)(2,1)} async-done(((bf16[2,512,2048]{2,1,0:T(8,128)(2,1)}), bf16[2,512,256]{2,1,0:T(8,128)(2,1)}) %reduce-scatter.27.cloned.1.call-update) | async-done | bytes 524304 | tf_op jit(solution)/shard_map/reduce_scatter | solution.py:339
  (571 shorter events, 274.2 us)
Async XLA Ops:
  7.2 80.8 %all-gather.21.cloned.1.call-start = ((), (), s32[]{:S(2)}) async-start(), calls=%async_computation.26 | async-start | bytes 1769472 | tf_op jit(solution)/shard_map/all_gather | solution.py:53
  9.1 174.3 %all-gather.23.cloned.1.call-start = ((), (), s32[]{:S(2)}) async-start(), calls=%async_computation.27 | async-start | bytes 4718592 | tf_op jit(solution)/shard_map/all_gather | solution.py:60
  11.5 181.1 %all-gather.25.cloned.1.call-start = ((), (), s32[]{:S(2)}) async-start(), calls=%async_computation.28 | async-start | bytes 4718592 | tf_op jit(solution)/shard_map/all_gather | solution.py:61
  12.6 229.4 %all-gather.27.cloned.1.call-start = ((), (), s32[]{:S(2)}) async-start(), calls=%async_computation.29 | async-start | bytes 1769472 | tf_op jit(solution)/shard_map/all_gather | solution.py:53
  13.2 293.7 %all-gather.29.cloned.1.call-start = ((), (), s32[]{:S(2)}) async-start(), calls=%async_computation.30 | async-start | bytes 4718592 | tf_op jit(solution)/shard_map/all_gather | solution.py:60
  13.8 302.3 %all-gather.31.cloned.1.call-start = ((), (), s32[]{:S(2)}) async-start(), calls=%async_computation.31 | async-start | bytes 4718592 | tf_op jit(solution)/shard_map/all_gather | solution.py:61
  14.5 22.5 %copy-start.132 = (bf16[2,2,64]{2,1,0:T(2,128)(2,1)S(1)}, bf16[2,2,64]{2,1,0:T(2,128)(2,1)}, u32[]{:S(2)}) copy-start(bf16[2,2,64]{2,1,0:T(2,128)(2,1)} %param.18) | copy-start | bytes 1540
  15.7 39.6 %copy-start.57 = (bf16[2,64,512]{2,1,0:T(8,128)(2,1)S(1)}, bf16[2,64,512]{2,1,0:T(8,128)(2,1)}, u32[]{:S(2)}) copy-start(bf16[2,64,512]{2,1,0:T(8,128)(2,1)} %param.15) | copy-start | bytes 393220
  33.8 47.3 %copy-start.110 = (s32[2,2,197,2]{2,3,1,0:T(2,128)S(1)}, s32[2,2,197,2]{2,3,1,0:T(2,128)}, u32[]{:S(2)}) copy-start(s32[2,2,197,2]{2,3,1,0:T(2,128)} %param.21) | copy-start | bytes 18916
  33.9 50.2 %copy-start.130 = (bf16[2,64,8]{1,2,0:T(8,128)(2,1)S(1)}, bf16[2,64,8]{1,2,0:T(8,128)(2,1)}, u32[]{:S(2)}) copy-start(bf16[2,64,8]{1,2,0:T(8,128)(2,1)} %param.16) | copy-start | bytes 6148
  36.6 53.7 %copy-start.94 = (f32[512]{0:T(512)}, f32[512]{0:T(512)S(1)}, u32[]{:S(2)}) copy-start(f32[512]{0:T(512)S(1)} %get-tuple-element.80) | copy-start | bytes 6148
  36.6 72.6 %copy-start.100 = (f32[512]{0:T(512)}, f32[512]{0:T(512)S(1)}, u32[]{:S(2)}) copy-start(f32[512]{0:T(512)S(1)} %get-tuple-element.79) | copy-start | bytes 6148
  36.7 53.6 %copy-start.8 = (f32[394,512]{1,0:T(8,128)}, f32[394,512]{1,0:T(8,128)S(1)}, u32[]{:S(2)}) copy-start(f32[394,512]{1,0:T(8,128)S(1)} %reshape.331) | copy-start | bytes 2420740
  36.9 53.4 %copy-start.78 = (f32[394]{0:T(512)}, f32[394]{0:T(512)S(1)}, u32[]{:S(2)}) copy-start(f32[394]{0:T(512)S(1)} %rsqrt.40) | copy-start | bytes 4732
  37.0 53.3 %copy-start.80 = (f32[394]{0:T(512)}, f32[394]{0:T(512)S(1)}, u32[]{:S(2)}) copy-start(f32[394]{0:T(512)S(1)} %div.51) | copy-start | bytes 4732
  55.3 35.1 %copy-start.104 = (f32[512]{0:T(512)}, f32[512]{0:T(512)S(1)}, u32[]{:S(2)}) copy-start(f32[512]{0:T(512)S(1)} %get-tuple-element.82) | copy-start | bytes 6148
  83.4 26.6 %copy-start.116 = (s32[394]{0:T(512)}, s32[394]{0:T(512)S(1)}, u32[]{:S(2)}) copy-start(s32[394]{0:T(512)S(1)} %get-tuple-element.110) | copy-start | bytes 4732
  83.4 26.6 %copy-start.118 = (s32[394]{0:T(512)}, s32[394]{0:T(512)S(1)}, u32[]{:S(2)}) copy-start(s32[394]{0:T(512)S(1)} %get-tuple-element.168) | copy-start | bytes 4732
  118.6 64.8 %all-to-all-start = ((bf16[4,2,147,512]{3,1,2,0:T(2,128)(2,1)}), bf16[4,2,147,512]{3,1,2,0:T(2,128)(2,1)}, u32[]{:S(2)}, u32[]{:S(2)}) async-start(bf16[4,2,147,512]{3,1,2,0:T(2,128)(2,1)} %copy.273), calls=%async_computation | async-start | bytes 2408448 | tf_op jit(solution)/shard_map/all_to_all | solution.py:102
  182.2 59.8 %copy-start.106 = (f32[512]{0:T(512)}, f32[512]{0:T(512)S(1)}, u32[]{:S(2)}) copy-start(f32[512]{0:T(512)S(1)} %get-tuple-element.78) | copy-start | bytes 6148
  183.4 90.3 %copy-start.112 = (s32[394]{0:T(512)}, s32[394]{0:T(512)S(1)}, u32[]{:S(2)}) copy-start(s32[394]{0:T(512)S(1)} %get-tuple-element.104) | copy-start | bytes 4732
  199.1 24.7 %copy-start.71 = (bf16[1,512,8]{1,2,0:T(8,128)(2,1)S(1)}, bf16[1,512,8]{1,2,0:T(8,128)(2,1)}, u32[]{:S(2)}) copy-start(bf16[1,512,8]{1,2,0:T(8,128)(2,1)} %copy.271) | copy-start | bytes 24580
  199.1 26.0 %copy-start.59 = (s32[394,1]{0,1:T(1,128)S(1)}, s32[394,1]{0,1:T(1,128)}, u32[]{:S(2)}) copy-start(s32[394,1]{0,1:T(1,128)} %copy-done.58) | copy-start | bytes 4732
  199.2 26.0 %copy-start.62 = (s32[394,1]{0,1:T(1,128)S(1)}, s32[394,1]{0,1:T(1,128)}, u32[]{:S(2)}) copy-start(s32[394,1]{0,1:T(1,128)} %copy-done.61) | copy-start | bytes 4732
  201.4 23.8 %all-to-all-start.1 = ((bf16[4,2,147,512]{3,1,2,0:T(2,128)(2,1)}), bf16[4,2,147,512]{3,1,2,0:T(2,128)(2,1)}, u32[]{:S(2)}, u32[]{:S(2)}) async-start(bf16[4,2,147,512]{3,1,2,0:T(2,128)(2,1)} %copy.275), calls=%async_computation.1 | async-start | bytes 2408448 | tf_op jit(solution)/shard_map/all_to_all | solution.py:110
  206.3 67.3 %copy-start.114 = (s32[394]{0:T(512)}, s32[394]{0:T(512)S(1)}, u32[]{:S(2)}) copy-start(s32[394]{0:T(512)S(1)} %get-tuple-element.106) | copy-start | bytes 4732
  282.2 24.7 %all-to-all-start.2 = ((bf16[4,2,147,512]{3,1,2,0:T(2,128)(2,1)}), bf16[4,2,147,512]{3,1,2,0:T(2,128)(2,1)}, u32[]{:S(2)}, u32[]{:S(2)}) async-start(bf16[4,2,147,512]{3,1,2,0:T(2,128)(2,1)} %copy.290), calls=%async_computation.2 | async-start | bytes 2408448 | tf_op jit(solution)/shard_map/all_to_all | solution.py:102
  324.8 20.7 %all-to-all-start.3 = ((bf16[4,2,147,512]{3,1,2,0:T(2,128)(2,1)}), bf16[4,2,147,512]{3,1,2,0:T(2,128)(2,1)}, u32[]{:S(2)}, u32[]{:S(2)}) async-start(bf16[4,2,147,512]{3,1,2,0:T(2,128)(2,1)} %copy.292), calls=%async_computation.3 | async-start | bytes 2408448 | tf_op jit(solution)/shard_map/all_to_all | solution.py:110
  367.4 21.2 %copy-start.136 = (bf16[1,2,2048,512]{3,2,1,0:T(8,128)(2,1)S(1)}, bf16[1,2,2048,512]{3,2,1,0:T(8,128)(2,1)}, u32[]{:S(2)}) copy-start(bf16[1,2,2048,512]{3,2,1,0:T(8,128)(2,1)} %all-gather.31.cloned.1.call-done) | copy-start | bytes 12582916
  401.8 18.8 %all-to-all-start.5 = ((bf16[4,2,147,512]{3,1,2,0:T(2,128)(2,1)}), bf16[4,2,147,512]{3,1,2,0:T(2,128)(2,1)}, u32[]{:S(2)}, u32[]{:S(2)}) async-start(bf16[4,2,147,512]{3,1,2,0:T(2,128)(2,1)} %copy.297), calls=%async_computation.5 | async-start | bytes 2408448 | tf_op jit(solution)/shard_map/all_to_all | solution.py:214
  502.6 18.2 %all-to-all-start.7 = ((bf16[4,2,147,512]{3,1,2,0:T(2,128)(2,1)}), bf16[4,2,147,512]{3,1,2,0:T(2,128)(2,1)}, u32[]{:S(2)}, u32[]{:S(2)}) async-start(bf16[4,2,147,512]{3,1,2,0:T(2,128)(2,1)} %copy.313), calls=%async_computation.7 | async-start | bytes 2408448 | tf_op jit(solution)/shard_map/all_to_all | solution.py:214
  507.1 62.2 %reduce-scatter.41.cloned.1.call-start = ((), (), s32[]{:S(2)}) async-start(), calls=%async_computation.35 | async-start | bytes 589824 | tf_op jit(solution)/shard_map/reduce_scatter | solution.py:325
  509.7 64.6 %reduce-scatter.39.cloned.1.call-start = ((), (), s32[]{:S(2)}) async-start(), calls=%async_computation.34 | async-start | bytes 589824 | tf_op jit(solution)/shard_map/reduce_scatter | solution.py:325
  532.0 77.4 %reduce-scatter.37.cloned.1.call-start = ((), (), s32[]{:S(2)}) async-start(), calls=%async_computation.33 | async-start | bytes 1769472 | tf_op jit(solution)/shard_map/reduce_scatter | solution.py:322
  536.1 108.0 %reduce-scatter.35.cloned.1.call-start = ((), (), s32[]{:S(2)}) async-start(), calls=%async_computation.32 | async-start | bytes 1769472 | tf_op jit(solution)/shard_map/reduce_scatter | solution.py:322
  560.0 119.7 %reduce-scatter.45.cloned.1.call-start = ((), (), s32[]{:S(2)}) async-start(), calls=%async_computation.37 | async-start | bytes 147456
  561.0 145.8 %reduce-scatter.53.cloned.1.call-start = ((), (), s32[]{:S(2)}) async-start(), calls=%async_computation.41 | async-start | bytes 147456
  561.9 176.5 %reduce-scatter.49.cloned.1.call-start = ((), (), s32[]{:S(2)}) async-start(), calls=%async_computation.39 | async-start | bytes 147456
  562.9 207.0 %reduce-scatter.43.cloned.1.call-start = ((), (), s32[]{:S(2)}) async-start(), calls=%async_computation.36 | async-start | bytes 147456
  563.9 236.8 %reduce-scatter.51.cloned.1.call-start = ((), (), s32[]{:S(2)}) async-start(), calls=%async_computation.40 | async-start | bytes 147456
  568.2 263.8 %reduce-scatter.47.cloned.1.call-start = ((), (), s32[]{:S(2)}) async-start(), calls=%async_computation.38 | async-start | bytes 147456
  569.1 309.9 %all-reduce.6.cloned.1.call-start = ((), (), s32[]{:S(2)}) async-start(), calls=%async_computation.42 | async-start | bytes 1048576 | tf_op jit(solution)/shard_map/psum | solution.py:315
  644.1 287.0 %reduce-scatter.33.cloned.1.call-start = ((), (), s32[]{:S(2)}) async-start(), calls=%async_computation.25 | async-start | bytes 4718592 | tf_op jit(solution)/shard_map/reduce_scatter | solution.py:342
  652.8 329.1 %reduce-scatter.31.cloned.1.call-start = ((), (), s32[]{:S(2)}) async-start(), calls=%async_computation.24 | async-start | bytes 4718592 | tf_op jit(solution)/shard_map/reduce_scatter | solution.py:342
  662.6 369.8 %reduce-scatter.29.cloned.1.call-start = ((), (), s32[]{:S(2)}) async-start(), calls=%async_computation.23 | async-start | bytes 4718592 | tf_op jit(solution)/shard_map/reduce_scatter | solution.py:339
  671.0 412.1 %reduce-scatter.27.cloned.1.call-start = ((), (), s32[]{:S(2)}) async-start(), calls=%async_computation.22 | async-start | bytes 4718592 | tf_op jit(solution)/shard_map/reduce_scatter | solution.py:339
  679.6 91.0 %copy-start.13 = (f32[394,512]{1,0:T(8,128)S(1)}, f32[394,512]{1,0:T(8,128)}, u32[]{:S(2)}) copy-start(f32[394,512]{1,0:T(8,128)} %copy-done.12) | copy-start | bytes 2420740
  679.6 91.0 %copy-start.49 = (f32[394,512]{1,0:T(8,128)S(1)}, f32[394,512]{1,0:T(8,128)}, u32[]{:S(2)}) copy-start(f32[394,512]{1,0:T(8,128)} %get-tuple-element.166) | copy-start | bytes 2420740
  (118 other events, 428.8 us)
Sparse Core Ops, SparseCore 0:
  10.2 29.4 all-gather.20
  41.3 51.4 all-gather.22
  94.4 47.3 all-gather.24
  143.9 25.8 all-gather.26
  171.2 49.7 all-gather.28
  222.4 45.8 all-gather.30
  510.1 32.3 reduce-scatter.40
  544.8 29.4 reduce-scatter.38
  577.2 32.1 reduce-scatter.36
  611.6 32.4 reduce-scatter.34
  646.9 28.9 reduce-scatter.44
  678.1 28.7 reduce-scatter.52
  709.6 28.7 reduce-scatter.48
  741.1 28.7 reduce-scatter.42
  771.9 28.7 reduce-scatter.50
  803.4 28.6 reduce-scatter.46
  835.2 43.8 all-reduce.5
  881.2 49.8 reduce-scatter.32
  933.4 48.3 reduce-scatter.30
  984.0 48.3 reduce-scatter.28
  1034.7 48.3 reduce-scatter.26
where the time goes:
time: 1100 us; the launch traced here: 1090 us
  waiting for transfers between devices  495 us (45%)
  local copies, waits for them, and re-layouts  186 us (17%)
  blocking collectives  182 us (17%)
  matrix products  151 us (14%)
  other arithmetic  35 us (3%)
  starting transfers between devices  27.2 us (2%)
  between operations  16.6 us (2%)
    unnamed x27, waiting for transfers between devices  147 us
    reduce_scatter x2, waiting for transfers between devices, body(): lax.psum_scatter(expert_part[1].astype(jnp.bfloat16), 'dp', scatter_dimen...  99.3 us
    reduce_scatter x2, waiting for transfers between devices, body(): lax.psum_scatter(expert_part[0].astype(jnp.bfloat16), 'dp', scatter_dimen...  98.6 us
    reduce_scatter x2, waiting for transfers between devices, body(): lax.psum_scatter(totals[0].astype(jnp.bfloat16), 'dp', scatter_dimension=...  69.8 us
    all_gather x2, blocking collectives, layer_forward(): lax.all_gather(w_proj[which], 'dp', axis=0, tiled=True)  42.8 us
    all_to_all x2, blocking collectives, layer_backward(): lax.all_to_all(slot_grads, 'expert', split_axis=0, concat_axis=0, tiled=T...  37.3 us
    psum x1, waiting for transfers between devices, body(): lax.psum(dense[0].astype(jnp.bfloat16), 'expert').astype(jnp.float32)  34.3 us
    unnamed x304, local copies, waits for them, and re-layouts  32.4 us
  transfers between devices with their start and end apart: 27, of which 16 were waited for; matrix products, arithmetic and copies ran while one was open for 23% of the time, Pallas kernels for 0%

commit v1 on v0

--- a/solution.py
+++ b/solution.py
@@ -312,7 +312,9 @@
         )
         grad, dense, expert_part = layer_backward(grad, saved)
         totals = (
-            lax.psum(dense[0].astype(jnp.bfloat16), "expert").astype(jnp.float32),
+            jnp.sum(lax.all_gather(dense[0].astype(jnp.bfloat16), "expert"), axis=0).astype(
+                jnp.float32
+            ),
             lax.psum(dense[1].astype(jnp.bfloat16), "expert").astype(jnp.float32),
             lax.psum(dense[2].astype(jnp.bfloat16), "expert").astype(jnp.float32),
             lax.psum(dense[3].astype(jnp.bfloat16), "expert").astype(jnp.float32),

time: 1100 us -> 1240 us (1.13)
  waiting for transfers between devices: 495 us -> 623 us
    all_gather x0 -> x2, waiting for transfers between devices: none -> 100 us  [body(): lax.all_gather(dense[0].astype(jnp.bfloat16), 'expert')]
    unnamed x27 -> x29, waiting for transfers between devices: 147 us -> 179 us
  transfers between devices with their start and end apart: 27 -> 29, of which waited for: 16 -> 19; matrix products, arithmetic and copies ran while one was open for 23% -> 21% of each run, Pallas kernels for 0% -> 0%
where the time goes in v1:
time: 1240 us; the launch traced here: 1230 us
  waiting for transfers between devices  623 us (50%)
  local copies, waits for them, and re-layouts  187 us (15%)
  blocking collectives  182 us (15%)
  matrix products  151 us (12%)
  other arithmetic  45.8 us (4%)
  starting transfers between devices  27.4 us (2%)
  between operations  16.3 us (1%)
    unnamed x29, waiting for transfers between devices  179 us
    reduce_scatter x2, waiting for transfers between devices, body(): lax.psum_scatter(expert_part[1].astype(jnp.bfloat16), 'dp', scatter_dimen...  101 us
    all_gather x2, waiting for transfers between devices, body(): lax.all_gather(dense[0].astype(jnp.bfloat16), 'expert')  100 us
    reduce_scatter x2, waiting for transfers between devices, body(): lax.psum_scatter(expert_part[0].astype(jnp.bfloat16), 'dp', scatter_dimen...  98.6 us
    reduce_scatter x2, waiting for transfers between devices, body(): lax.psum_scatter(totals[0].astype(jnp.bfloat16), 'dp', scatter_dimension=...  67.2 us
    all_gather x2, blocking collectives, layer_forward(): lax.all_gather(w_proj[which], 'dp', axis=0, tiled=True)  40.2 us
    all_to_all x2, blocking collectives, layer_backward(): lax.all_to_all(slot_grads, 'expert', split_axis=0, concat_axis=0, tiled=T...  36.8 us
    all_gather x2, blocking collectives, layer_forward(): lax.all_gather(w_router[which], 'dp', axis=0, tiled=True)  32.6 us
  transfers between devices with their start and end apart: 29, of which 19 were waited for; matrix products, arithmetic and copies ran while one was open for 21% of the time, Pallas kernels for 0%

profile of v1, /device:TPU:0, one launch (start us, length us, event | category | flops | bytes accessed | tf_op | source)
XLA Modules:
  0.0 1232.4 jit_solution(3108778533894409035)
XLA Ops:
  16.5 17.0 %all-gather = bf16[1,2,512]{1,0,2:T(2,128)(2,1)S(1)} all-gather(bf16[1,2,64]{1,0,2:T(2,128)(2,1)S(1)} %copy.377), channel_id=2, replica_groups=mesh['dp'=8,'expert'=4] {'dp'}, dimensions={2}, use_global_device_ids=true | all-gather | bytes 2304 | tf_op jit(solution)/shard_map/all_gather | solution.py:56
  37.7 14.6 %all-gather.1 = bf16[1,2,512]{1,0,2:T(2,128)(2,1)S(1)} all-gather(bf16[1,2,64]{1,0,2:T(2,128)(2,1)S(1)} %copy.378), channel_id=3, replica_groups=mesh['dp'=8,'expert'=4] {'dp'}, dimensions={2}, use_global_device_ids=true | all-gather | bytes 2304 | tf_op jit(solution)/shard_map/all_gather | solution.py:57
  55.9 20.8 %all-gather.3 = bf16[1,512,512]{2,1,0:T(8,128)(2,1)} all-gather(bf16[1,64,512]{2,1,0:T(8,128)(2,1)S(1)} %get-tuple-element.124), channel_id=5, replica_groups=mesh['dp'=8,'expert'=4] {'dp'}, dimensions={1}, use_global_device_ids=true | all-gather | bytes 589824 | tf_op jit(solution)/shard_map/all_gather | solution.py:54
  114.1 4.3 all-to-all-start
  118.4 17.5 %all-gather.4 = bf16[1,512,8]{2,0,1:T(2,128)(2,1)S(1)} all-gather(bf16[1,64,8]{2,0,1:T(2,128)(2,1)} %copy.379), channel_id=6, replica_groups=mesh['dp'=8,'expert'=4] {'dp'}, dimensions={1}, use_global_device_ids=true | all-gather | bytes 9216 | tf_op jit(solution)/shard_map/all_gather | solution.py:55
  137.4 14.6 %all-gather.7 = bf16[1,2,512]{1,0,2:T(2,128)(2,1)S(1)} all-gather(bf16[1,2,64]{1,0,2:T(2,128)(2,1)S(1)} %copy.380), channel_id=9, replica_groups=mesh['dp'=8,'expert'=4] {'dp'}, dimensions={2}, use_global_device_ids=true | all-gather | bytes 2304 | tf_op jit(solution)/shard_map/all_gather | solution.py:56
  153.6 15.8 %all-gather.8 = bf16[1,2,512]{1,0,2:T(2,128)(2,1)S(1)} all-gather(bf16[1,2,64]{1,0,2:T(2,128)(2,1)} %copy.381), channel_id=10, replica_groups=mesh['dp'=8,'expert'=4] {'dp'}, dimensions={2}, use_global_device_ids=true | all-gather | bytes 2304 | tf_op jit(solution)/shard_map/all_gather | solution.py:57
  181.5 9.1 fusion.17
  190.6 6.4 fusion.77
  204.2 19.4 %all-gather.10 = bf16[1,512,512]{2,1,0:T(8,128)(2,1)} all-gather(bf16[1,64,512]{2,1,0:T(8,128)(2,1)S(1)} %copy-done.50), channel_id=12, replica_groups=mesh['dp'=8,'expert'=4] {'dp'}, dimensions={1}, use_global_device_ids=true | all-gather | bytes 589824 | tf_op jit(solution)/shard_map/all_gather | solution.py:54
  230.3 4.5 gather_fusion
  282.2 4.3 all-to-all-start.2
  287.2 15.1 %all-gather.11 = bf16[1,512,8]{2,0,1:T(2,128)(2,1)S(1)} all-gather(bf16[1,64,8]{2,0,1:T(2,128)(2,1)} %copy.382), channel_id=13, replica_groups=mesh['dp'=8,'expert'=4] {'dp'}, dimensions={1}, use_global_device_ids=true | all-gather | bytes 9216 | tf_op jit(solution)/shard_map/all_gather | solution.py:55
  307.2 9.1 fusion.13
  316.3 6.4 fusion.83
  325.0 4.3 all-to-all-start.3
  330.7 14.8 %all-to-all-done.3 = bf16[4,2,147,512]{3,1,2,0:T(2,128)(2,1)} async-done(((bf16[4,2,147,512]{3,1,2,0:T(2,128)(2,1)}), bf16[4,2,147,512]{3,1,2,0:T(2,128)(2,1)}, u32[]{:S(2)}, u32[]{:S(2)}) %all-to-all-start.3) | async-done | bytes 1204256 | tf_op jit(solution)/shard_map/all_to_all | solution.py:110
  369.8 18.6 %all_to_all.44 = bf16[4,2,147,512]{3,1,2,0:T(2,128)(2,1)S(1)} all-to-all(bf16[4,2,147,512]{3,1,2,0:T(2,128)(2,1)S(1)} %copy.295), channel_id=1, replica_groups=mesh['dp'=8,'expert'=4] {'expert'}, dimensions={0} | all-to-all | bytes 2408448 | tf_op jit(solution)/shard_map/all_to_all | solution.py:200
  388.4 8.1 fusion.5
  401.6 4.3 all-to-all-start.5
  405.9 13.9 %all-to-all-done.5 = bf16[4,2,147,512]{3,1,2,0:T(2,128)(2,1)} async-done(((bf16[4,2,147,512]{3,1,2,0:T(2,128)(2,1)}), bf16[4,2,147,512]{3,1,2,0:T(2,128)(2,1)}, u32[]{:S(2)}, u32[]{:S(2)}) %all-to-all-start.5) | async-done | bytes 1204256 | tf_op jit(solution)/shard_map/all_to_all | solution.py:214
  470.5 18.2 %all_to_all.45 = bf16[4,2,147,512]{3,1,2,0:T(2,128)(2,1)S(1)} all-to-all(bf16[4,2,147,512]{3,1,2,0:T(2,128)(2,1)S(1)} %copy.311), channel_id=1, replica_groups=mesh['dp'=8,'expert'=4] {'expert'}, dimensions={0} | all-to-all | bytes 2408448 | tf_op jit(solution)/shard_map/all_to_all | solution.py:200
  488.6 8.1 fusion.11
  501.8 4.4 all-to-all-start.7
  509.0 11.1 all-to-all-done.7
  568.5 6.2 reduce-scatter.39.cloned.1.call-done
  575.1 8.5 bitcast_convert_fusion
  585.0 8.7 bitcast_convert_fusion.1
  593.9 8.3 bitcast_convert_fusion.2
  602.4 8.6 bitcast_convert_fusion.3
  611.1 34.1 %all-gather.39.cloned.1.call-done = bf16[2048,1536]{1,0:T(8,128)(2,1)} async-done(((bf16[512,1536]{1,0:T(8,128)(2,1)}), bf16[2048,1536]{1,0:T(8,128)(2,1)}) %all-gather.39.cloned.1.call-update) | async-done | bytes 6291472 | tf_op jit(solution)/shard_map/all_gather | solution.py:315
  645.2 5.4 reduce_sum.537
  650.7 66.3 %all-gather.37.cloned.1.call-done = bf16[2048,1536]{1,0:T(8,128)(2,1)} async-done(((bf16[512,1536]{1,0:T(8,128)(2,1)}), bf16[2048,1536]{1,0:T(8,128)(2,1)}) %all-gather.37.cloned.1.call-update) | async-done | bytes 6291472 | tf_op jit(solution)/shard_map/all_gather | solution.py:315
  717.0 5.4 reduce_sum.536
  722.4 28.0 %reduce-scatter.45.cloned.1.call-done = bf16[64,8]{1,0:T(8,128)(2,1)} async-done(((bf16[512,8]{1,0:T(8,128)(2,1)}), bf16[64,8]{1,0:T(8,128)(2,1)}) %reduce-scatter.45.cloned.1.call-update) | async-done | bytes 1040
  752.3 28.9 %reduce-scatter.53.cloned.1.call-done = bf16[64,2]{1,0:T(8,128)(2,1)} async-done(((bf16[512,2]{1,0:T(8,128)(2,1)}), bf16[64,2]{1,0:T(8,128)(2,1)}) %reduce-scatter.53.cloned.1.call-update) | async-done | bytes 272
  782.0 30.8 %reduce-scatter.49.cloned.1.call-done = bf16[64,2]{1,0:T(8,128)(2,1)} async-done(((bf16[512,2]{1,0:T(8,128)(2,1)}), bf16[64,2]{1,0:T(8,128)(2,1)}) %reduce-scatter.49.cloned.1.call-update) | async-done | bytes 272
  813.6 30.6 %reduce-scatter.43.cloned.1.call-done = bf16[64,8]{1,0:T(8,128)(2,1)} async-done(((bf16[512,8]{1,0:T(8,128)(2,1)}), bf16[64,8]{1,0:T(8,128)(2,1)}) %reduce-scatter.43.cloned.1.call-update) | async-done | bytes 1040
  847.0 28.1 %reduce-scatter.51.cloned.1.call-done = bf16[64,2]{1,0:T(8,128)(2,1)} async-done(((bf16[512,2]{1,0:T(8,128)(2,1)}), bf16[64,2]{1,0:T(8,128)(2,1)}) %reduce-scatter.51.cloned.1.call-update) | async-done | bytes 272
  875.8 30.7 %reduce-scatter.47.cloned.1.call-done = bf16[64,2]{1,0:T(8,128)(2,1)} async-done(((bf16[512,2]{1,0:T(8,128)(2,1)}), bf16[64,2]{1,0:T(8,128)(2,1)}) %reduce-scatter.47.cloned.1.call-update) | async-done | bytes 272
  907.3 10.0 all-reduce.2
  919.1 30.6 %all-reduce.6.cloned.1.call-done = (bf16[64,512]{1,0:T(8,128)(2,1)}, bf16[64,512]{1,0:T(8,128)(2,1)}) async-done(((bf16[64,512]{1,0:T(8,128)(2,1)}, bf16[64,512]{1,0:T(8,128)(2,1)}), (bf16[64,512]{1,0:T(8,128)(2,1)}, bf16[64,512]{1,0:T(8,128)(2,1)})) %all-reduce.6.cloned.1.call-update) | async-done | bytes 131088 | tf_op jit(solution)/shard_map/psum | solution.py:318
  951.3 50.5 %reduce-scatter.37.cloned.1.call-done = bf16[2,256,512]{2,1,0:T(8,128)(2,1)} async-done(((bf16[2,2048,512]{2,1,0:T(8,128)(2,1)}), bf16[2,256,512]{2,1,0:T(8,128)(2,1)}) %reduce-scatter.37.cloned.1.call-update) | async-done | bytes 524304 | tf_op jit(solution)/shard_map/reduce_scatter | solution.py:344
  1001.8 50.7 %reduce-scatter.35.cloned.1.call-done = bf16[2,256,512]{2,1,0:T(8,128)(2,1)} async-done(((bf16[2,2048,512]{2,1,0:T(8,128)(2,1)}), bf16[2,256,512]{2,1,0:T(8,128)(2,1)}) %reduce-scatter.35.cloned.1.call-update) | async-done | bytes 524304 | tf_op jit(solution)/shard_map/reduce_scatter | solution.py:344
  1055.2 47.9 %reduce-scatter.33.cloned.1.call-done = bf16[2,512,256]{2,1,0:T(8,128)(2,1)} async-done(((bf16[2,512,2048]{2,1,0:T(8,128)(2,1)}), bf16[2,512,256]{2,1,0:T(8,128)(2,1)}) %reduce-scatter.33.cloned.1.call-update) | async-done | bytes 524304 | tf_op jit(solution)/shard_map/reduce_scatter | solution.py:341
  1103.1 50.7 %reduce-scatter.31.cloned.1.call-done = bf16[2,512,256]{2,1,0:T(8,128)(2,1)} async-done(((bf16[2,512,2048]{2,1,0:T(8,128)(2,1)}), bf16[2,512,256]{2,1,0:T(8,128)(2,1)}) %reduce-scatter.31.cloned.1.call-update) | async-done | bytes 524304 | tf_op jit(solution)/shard_map/reduce_scatter | solution.py:341
  1156.5 32.3 %reduce-scatter.29.cloned.1.call-done = bf16[64,1536]{1,0:T(8,128)(2,1)} async-done(((bf16[512,1536]{1,0:T(8,128)(2,1)}), bf16[64,1536]{1,0:T(8,128)(2,1)}) %reduce-scatter.29.cloned.1.call-update) | async-done | bytes 196624 | tf_op jit(solution)/shard_map/reduce_scatter | solution.py:324
  1188.8 34.9 %reduce-scatter.27.cloned.1.call-done = bf16[64,1536]{1,0:T(8,128)(2,1)} async-done(((bf16[512,1536]{1,0:T(8,128)(2,1)}), bf16[64,1536]{1,0:T(8,128)(2,1)}) %reduce-scatter.27.cloned.1.call-update) | async-done | bytes 196624 | tf_op jit(solution)/shard_map/reduce_scatter | solution.py:324
  (579 shorter events, 295.1 us)
Async XLA Ops:
  7.2 76.4 %all-gather.25.cloned.1.call-start = ((), (), s32[]{:S(2)}) async-start(), calls=%async_computation.28 | async-start | bytes 1769472 | tf_op jit(solution)/shard_map/all_gather | solution.py:53
  9.1 172.3 %all-gather.27.cloned.1.call-start = ((), (), s32[]{:S(2)}) async-start(), calls=%async_computation.29 | async-start | bytes 4718592 | tf_op jit(solution)/shard_map/all_gather | solution.py:60
  11.5 179.1 %all-gather.29.cloned.1.call-start = ((), (), s32[]{:S(2)}) async-start(), calls=%async_computation.30 | async-start | bytes 4718592 | tf_op jit(solution)/shard_map/all_gather | solution.py:61
  12.6 229.4 %all-gather.31.cloned.1.call-start = ((), (), s32[]{:S(2)}) async-start(), calls=%async_computation.31 | async-start | bytes 1769472 | tf_op jit(solution)/shard_map/all_gather | solution.py:53
  13.2 294.0 %all-gather.33.cloned.1.call-start = ((), (), s32[]{:S(2)}) async-start(), calls=%async_computation.32 | async-start | bytes 4718592 | tf_op jit(solution)/shard_map/all_gather | solution.py:60
  13.8 302.5 %all-gather.35.cloned.1.call-start = ((), (), s32[]{:S(2)}) async-start(), calls=%async_computation.33 | async-start | bytes 4718592 | tf_op jit(solution)/shard_map/all_gather | solution.py:61
  15.7 39.6 %copy-start.57 = (bf16[2,64,512]{2,1,0:T(8,128)(2,1)S(1)}, bf16[2,64,512]{2,1,0:T(8,128)(2,1)}, u32[]{:S(2)}) copy-start(bf16[2,64,512]{2,1,0:T(8,128)(2,1)} %param.15) | copy-start | bytes 393220
  33.8 42.9 %copy-start.110 = (s32[2,2,197,2]{2,3,1,0:T(2,128)S(1)}, s32[2,2,197,2]{2,3,1,0:T(2,128)}, u32[]{:S(2)}) copy-start(s32[2,2,197,2]{2,3,1,0:T(2,128)} %param.21) | copy-start | bytes 18916
  33.9 45.8 %copy-start.130 = (bf16[2,64,8]{1,2,0:T(8,128)(2,1)S(1)}, bf16[2,64,8]{1,2,0:T(8,128)(2,1)}, u32[]{:S(2)}) copy-start(bf16[2,64,8]{1,2,0:T(8,128)(2,1)} %param.16) | copy-start | bytes 6148
  36.6 49.3 %copy-start.94 = (f32[512]{0:T(512)}, f32[512]{0:T(512)S(1)}, u32[]{:S(2)}) copy-start(f32[512]{0:T(512)S(1)} %get-tuple-element.80) | copy-start | bytes 6148
  36.6 68.1 %copy-start.100 = (f32[512]{0:T(512)}, f32[512]{0:T(512)S(1)}, u32[]{:S(2)}) copy-start(f32[512]{0:T(512)S(1)} %get-tuple-element.79) | copy-start | bytes 6148
  36.7 49.2 %copy-start.8 = (f32[394,512]{1,0:T(8,128)}, f32[394,512]{1,0:T(8,128)S(1)}, u32[]{:S(2)}) copy-start(f32[394,512]{1,0:T(8,128)S(1)} %reshape.331) | copy-start | bytes 2420740
  36.9 49.0 %copy-start.78 = (f32[394]{0:T(512)}, f32[394]{0:T(512)S(1)}, u32[]{:S(2)}) copy-start(f32[394]{0:T(512)S(1)} %rsqrt.40) | copy-start | bytes 4732
  37.0 48.9 %copy-start.80 = (f32[394]{0:T(512)}, f32[394]{0:T(512)S(1)}, u32[]{:S(2)}) copy-start(f32[394]{0:T(512)S(1)} %div.51) | copy-start | bytes 4732
  55.3 30.6 %copy-start.104 = (f32[512]{0:T(512)}, f32[512]{0:T(512)S(1)}, u32[]{:S(2)}) copy-start(f32[512]{0:T(512)S(1)} %get-tuple-element.82) | copy-start | bytes 6148
  79.0 26.5 %copy-start.118 = (s32[394]{0:T(512)}, s32[394]{0:T(512)S(1)}, u32[]{:S(2)}) copy-start(s32[394]{0:T(512)S(1)} %get-tuple-element.166) | copy-start | bytes 4732
  114.1 67.3 %all-to-all-start = ((bf16[4,2,147,512]{3,1,2,0:T(2,128)(2,1)}), bf16[4,2,147,512]{3,1,2,0:T(2,128)(2,1)}, u32[]{:S(2)}, u32[]{:S(2)}) async-start(bf16[4,2,147,512]{3,1,2,0:T(2,128)(2,1)} %copy.273), calls=%async_computation | async-start | bytes 2408448 | tf_op jit(solution)/shard_map/all_to_all | solution.py:102
  180.2 61.8 %copy-start.106 = (f32[512]{0:T(512)}, f32[512]{0:T(512)S(1)}, u32[]{:S(2)}) copy-start(f32[512]{0:T(512)S(1)} %get-tuple-element.78) | copy-start | bytes 6148
  181.4 92.2 %copy-start.112 = (s32[394]{0:T(512)}, s32[394]{0:T(512)S(1)}, u32[]{:S(2)}) copy-start(s32[394]{0:T(512)S(1)} %get-tuple-element.102) | copy-start | bytes 4732
  197.0 26.6 %copy-start.71 = (bf16[1,512,8]{1,2,0:T(8,128)(2,1)S(1)}, bf16[1,512,8]{1,2,0:T(8,128)(2,1)}, u32[]{:S(2)}) copy-start(bf16[1,512,8]{1,2,0:T(8,128)(2,1)} %copy.271) | copy-start | bytes 24580
  197.1 27.9 %copy-start.59 = (s32[394,1]{0,1:T(1,128)S(1)}, s32[394,1]{0,1:T(1,128)}, u32[]{:S(2)}) copy-start(s32[394,1]{0,1:T(1,128)} %copy-done.58) | copy-start | bytes 4732
  197.1 27.9 %copy-start.62 = (s32[394,1]{0,1:T(1,128)S(1)}, s32[394,1]{0,1:T(1,128)}, u32[]{:S(2)}) copy-start(s32[394,1]{0,1:T(1,128)} %copy-done.61) | copy-start | bytes 4732
  199.3 25.7 %all-to-all-start.1 = ((bf16[4,2,147,512]{3,1,2,0:T(2,128)(2,1)}), bf16[4,2,147,512]{3,1,2,0:T(2,128)(2,1)}, u32[]{:S(2)}, u32[]{:S(2)}) async-start(bf16[4,2,147,512]{3,1,2,0:T(2,128)(2,1)} %copy.275), calls=%async_computation.1 | async-start | bytes 2408448 | tf_op jit(solution)/shard_map/all_to_all | solution.py:110
  204.2 69.4 %copy-start.114 = (s32[394]{0:T(512)}, s32[394]{0:T(512)S(1)}, u32[]{:S(2)}) copy-start(s32[394]{0:T(512)S(1)} %get-tuple-element.104) | copy-start | bytes 4732
  282.2 25.0 %all-to-all-start.2 = ((bf16[4,2,147,512]{3,1,2,0:T(2,128)(2,1)}), bf16[4,2,147,512]{3,1,2,0:T(2,128)(2,1)}, u32[]{:S(2)}, u32[]{:S(2)}) async-start(bf16[4,2,147,512]{3,1,2,0:T(2,128)(2,1)} %copy.290), calls=%async_computation.2 | async-start | bytes 2408448 | tf_op jit(solution)/shard_map/all_to_all | solution.py:102
  325.0 20.4 %all-to-all-start.3 = ((bf16[4,2,147,512]{3,1,2,0:T(2,128)(2,1)}), bf16[4,2,147,512]{3,1,2,0:T(2,128)(2,1)}, u32[]{:S(2)}, u32[]{:S(2)}) async-start(bf16[4,2,147,512]{3,1,2,0:T(2,128)(2,1)} %copy.292), calls=%async_computation.3 | async-start | bytes 2408448 | tf_op jit(solution)/shard_map/all_to_all | solution.py:110
  401.6 18.2 %all-to-all-start.5 = ((bf16[4,2,147,512]{3,1,2,0:T(2,128)(2,1)}), bf16[4,2,147,512]{3,1,2,0:T(2,128)(2,1)}, u32[]{:S(2)}, u32[]{:S(2)}) async-start(bf16[4,2,147,512]{3,1,2,0:T(2,128)(2,1)} %copy.297), calls=%async_computation.5 | async-start | bytes 2408448 | tf_op jit(solution)/shard_map/all_to_all | solution.py:214
  501.8 18.3 %all-to-all-start.7 = ((bf16[4,2,147,512]{3,1,2,0:T(2,128)(2,1)}), bf16[4,2,147,512]{3,1,2,0:T(2,128)(2,1)}, u32[]{:S(2)}, u32[]{:S(2)}) async-start(bf16[4,2,147,512]{3,1,2,0:T(2,128)(2,1)} %copy.313), calls=%async_computation.7 | async-start | bytes 2408448 | tf_op jit(solution)/shard_map/all_to_all | solution.py:214
  506.3 62.2 %reduce-scatter.41.cloned.1.call-start = ((), (), s32[]{:S(2)}) async-start(), calls=%async_computation.37 | async-start | bytes 589824 | tf_op jit(solution)/shard_map/reduce_scatter | solution.py:327
  508.9 65.8 %reduce-scatter.39.cloned.1.call-start = ((), (), s32[]{:S(2)}) async-start(), calls=%async_computation.36 | async-start | bytes 589824 | tf_op jit(solution)/shard_map/reduce_scatter | solution.py:327
  531.2 114.0 %all-gather.39.cloned.1.call-start = ((), (), s32[]{:S(2)}) async-start(), calls=%async_computation.35 | async-start | bytes 7864320 | tf_op jit(solution)/shard_map/all_gather | solution.py:315
  535.3 181.6 %all-gather.37.cloned.1.call-start = ((), (), s32[]{:S(2)}) async-start(), calls=%async_computation.34 | async-start | bytes 7864320 | tf_op jit(solution)/shard_map/all_gather | solution.py:315
  559.2 191.2 %reduce-scatter.45.cloned.1.call-start = ((), (), s32[]{:S(2)}) async-start(), calls=%async_computation.39 | async-start | bytes 147456
  560.2 221.0 %reduce-scatter.53.cloned.1.call-start = ((), (), s32[]{:S(2)}) async-start(), calls=%async_computation.43 | async-start | bytes 147456
  561.2 251.6 %reduce-scatter.49.cloned.1.call-start = ((), (), s32[]{:S(2)}) async-start(), calls=%async_computation.41 | async-start | bytes 147456
  562.1 282.1 %reduce-scatter.43.cloned.1.call-start = ((), (), s32[]{:S(2)}) async-start(), calls=%async_computation.38 | async-start | bytes 147456
  563.1 311.9 %reduce-scatter.51.cloned.1.call-start = ((), (), s32[]{:S(2)}) async-start(), calls=%async_computation.42 | async-start | bytes 147456
  567.5 339.0 %reduce-scatter.47.cloned.1.call-start = ((), (), s32[]{:S(2)}) async-start(), calls=%async_computation.40 | async-start | bytes 147456
  568.4 381.3 %all-reduce.6.cloned.1.call-start = ((), (), s32[]{:S(2)}) async-start(), calls=%async_computation.44 | async-start | bytes 262144 | tf_op jit(solution)/shard_map/psum | solution.py:318
  574.7 427.1 %reduce-scatter.37.cloned.1.call-start = ((), (), s32[]{:S(2)}) async-start(), calls=%async_computation.27 | async-start | bytes 4718592 | tf_op jit(solution)/shard_map/reduce_scatter | solution.py:344
  583.7 468.8 %reduce-scatter.35.cloned.1.call-start = ((), (), s32[]{:S(2)}) async-start(), calls=%async_computation.26 | async-start | bytes 4718592 | tf_op jit(solution)/shard_map/reduce_scatter | solution.py:344
  593.8 509.3 %reduce-scatter.33.cloned.1.call-start = ((), (), s32[]{:S(2)}) async-start(), calls=%async_computation.25 | async-start | bytes 4718592 | tf_op jit(solution)/shard_map/reduce_scatter | solution.py:341
  602.2 551.6 %reduce-scatter.31.cloned.1.call-start = ((), (), s32[]{:S(2)}) async-start(), calls=%async_computation.24 | async-start | bytes 4718592 | tf_op jit(solution)/shard_map/reduce_scatter | solution.py:341
  611.0 577.8 %reduce-scatter.29.cloned.1.call-start = ((), (), s32[]{:S(2)}) async-start(), calls=%async_computation.23 | async-start | bytes 1769472 | tf_op jit(solution)/shard_map/reduce_scatter | solution.py:324
  650.7 573.0 %reduce-scatter.27.cloned.1.call-start = ((), (), s32[]{:S(2)}) async-start(), calls=%async_computation.22 | async-start | bytes 1769472 | tf_op jit(solution)/shard_map/reduce_scatter | solution.py:324
  717.0 34.2 %copy-start.42 = (bf16[394,512]{1,0:T(8,128)(2,1)S(1)}, bf16[394,512]{1,0:T(8,128)(2,1)}, u32[]{:S(2)}) copy-start(bf16[394,512]{1,0:T(8,128)(2,1)} %get-tuple-element.120) | copy-start | bytes 1210372
  722.3 122.7 %copy-start.13 = (f32[394,512]{1,0:T(8,128)S(1)}, f32[394,512]{1,0:T(8,128)}, u32[]{:S(2)}) copy-start(f32[394,512]{1,0:T(8,128)} %copy-done.12) | copy-start | bytes 2420740
  722.3 122.7 %copy-start.49 = (f32[394,512]{1,0:T(8,128)S(1)}, f32[394,512]{1,0:T(8,128)}, u32[]{:S(2)}) copy-start(f32[394,512]{1,0:T(8,128)} %get-tuple-element.164) | copy-start | bytes 2420740
  (120 other events, 498.3 us)
Sparse Core Ops, SparseCore 0:
  10.2 29.4 all-gather.24
  41.3 51.4 all-gather.26
  94.4 47.3 all-gather.28
  143.9 25.6 all-gather.30
  171.0 50.4 all-gather.32
  222.9 45.9 all-gather.34
  509.3 33.6 reduce-scatter.40
  545.3 29.3 reduce-scatter.38
  577.1 68.0 all-gather.38
  646.9 70.0 all-gather.36
  719.8 30.5 reduce-scatter.44
  752.5 28.7 reduce-scatter.52
  784.1 28.7 reduce-scatter.48
  815.5 28.7 reduce-scatter.42
  846.3 28.6 reduce-scatter.50
  877.7 28.7 reduce-scatter.46
  909.2 40.4 all-reduce.5
  951.9 49.8 reduce-scatter.36
  1004.1 48.3 reduce-scatter.34
  1054.7 48.3 reduce-scatter.32
  1105.4 48.3 reduce-scatter.30
  1156.1 32.6 reduce-scatter.28
  1191.1 32.5 reduce-scatter.26
